TPU v7x, 32 devices: a whole 2x2x4 slice. The times are simulated.
32 devices in a mesh: dom: 16 (over z, y, x), chan: 2 (over core).
Axes of the slice: x: 2, y: 2, z: 4, core: 2. Of those that a mesh axis runs over, the one named last changes fastest.
Arguments:
- features: bfloat16 [16384, 512], P('dom', 'chan'), may hold values from -6 to 6
- w_self: bfloat16 [512, 512], P('chan'), may hold values from -0.25 to 0.25
- w_neigh: bfloat16 [512, 512], P('chan'), may hold values from -1.5 to 1.5
- degrees: int32 [16384], P('dom'), may hold values from 16 to 48
- local_src: int32 [128], P('dom'), may hold values from 0 to 7
- local_dst: int32 [128], P('dom'), may hold values from 0 to 7
- local_tiles: bfloat16 [128, 128, 128], P('dom'), may hold values from 0 to 1, as said below
- remote_src: int32 [256], P('dom'), may hold values from 0 to 7
- remote_part: int32 [256, 1], P('dom'), may hold values from 0 to 15; in each aligned block of 16 rows (0 to 15, 16 to 31, ...) at most 2 rows name the same one
- remote_dst: int32 [256], P('dom'), may hold values from 0 to 7
- remote_tiles: bfloat16 [256, 128, 128], P('dom'), may hold values from 0 to 1, as said below
- cotangent: bfloat16 [16384, 512], P('dom', 'chan'), may hold values from -6 to 6
Outputs:
- output: bfloat16 [16384, 512], P('dom', 'chan')
- grad_self: float32 [512, 512], P('chan')
- grad_neigh: float32 [512, 512], P('chan')
- grad_features: bfloat16 [16384, 512], P('dom', 'chan')
Inputs may be any that keep to these rules, and one draw needn't show every extreme that they name: `remote_part`: among the 16 remote tiles of one partition each partition is named at most 2 times, a bound that some block reaches. `local_tiles`: every entry is 0 or 1. `remote_tiles`: every entry is 0 or 1.
All inputs are finite; a program needn't handle non-finite values.
Results may differ from a plain program's by a relative error of at most 0.015.
Values may be sent and summed in bfloat16 or wider, within the bound.
No kernel may reach another device: no remote copies, remote signals or barrier semaphores. Data moves between devices by JAX's collectives and lax.ppermute only.
A program may use at most 64 MiB of HBM per device.

v0:
```python
import math

import jax
import jax.numpy as jnp
from jax import lax
from jax.sharding import PartitionSpec as P

TILE = 128
CAP = 2


def silu_slope(value):
    sig = jax.nn.sigmoid(value)
    return sig * (1.0 + value * (1.0 - sig))


def tile_products(tiles, sources, feat_blocks):
    picked = jnp.take(feat_blocks, sources, axis=0)
    return jnp.einsum("tij,tic->tjc", tiles, picked, preferred_element_type=jnp.float32)


def local_sum(local_tiles, local_src, local_dst, feat_blocks, block_count):
    terms = tile_products(local_tiles, local_src, feat_blocks)
    onehot = (jnp.arange(block_count, dtype=jnp.int32)[:, None] == local_dst[None, :]).astype(
        jnp.float32
    )
    flat = terms.reshape(terms.shape[0], -1)
    return jnp.einsum("bt,tk->bk", onehot, flat, precision=lax.Precision.HIGHEST)


def push_partials(outgoing, out_blocks):
    return (
        lax.all_to_all(outgoing, "dom", split_axis=0, concat_axis=0, tiled=True),
        lax.all_to_all(out_blocks, "dom", split_axis=0, concat_axis=0, tiled=True),
    )


def per_device(
    features,
    w_self,
    w_neigh,
    degrees,
    local_src,
    local_dst,
    local_tiles,
    remote_src,
    remote_part,
    remote_dst,
    remote_tiles,
    cotangent,
):
    domains = lax.axis_size("dom")
    node_rows, channels = features.shape
    block_count = node_rows // TILE
    remote_count = remote_tiles.shape[0]
    slot_count = domains * CAP
    feat_blocks = features.reshape(block_count, TILE, channels)
    targets = remote_part[:, 0]
    counter = jnp.arange(remote_count, dtype=jnp.int32)
    same_before = (targets[:, None] == targets[None, :]) & (counter[None, :] < counter[:, None])
    position = jnp.sum(jnp.where(same_before, 1, 0), axis=1).astype(jnp.int32)
    slot_index = targets * CAP + position
    local_part = local_sum(local_tiles, local_src, local_dst, feat_blocks, block_count)
    pushed = tile_products(remote_tiles, remote_src, feat_blocks).astype(jnp.bfloat16)
    outgoing = jnp.zeros((slot_count, TILE * channels), jnp.bfloat16)
    outgoing = outgoing.at[slot_index].set(pushed.reshape(remote_count, TILE * channels))
    out_blocks = jnp.zeros((slot_count,), jnp.int32).at[slot_index].set(remote_dst)
    received, got_blocks = push_partials(
        outgoing.reshape(domains, CAP * TILE * channels), out_blocks.reshape(domains, CAP)
    )
    incoming = received.reshape(slot_count, TILE * channels)
    got_index = got_blocks.reshape(slot_count)
    onehot_in = (jnp.arange(block_count, dtype=jnp.int32)[:, None] == got_index[None, :]).astype(
        jnp.bfloat16
    )
    remote_part_sum = jnp.dot(onehot_in, incoming, preferred_element_type=jnp.float32)
    summed = (local_part + remote_part_sum).reshape(node_rows, channels)
    divisor = degrees.astype(jnp.float32)[:, None]
    averaged = (summed / divisor).astype(jnp.bfloat16)
    joined = jnp.concatenate([features, averaged], axis=1)
    weights = jnp.concatenate([w_self, w_neigh], axis=0)
    partial_value = jnp.dot(joined, weights, preferred_element_type=jnp.float32)
    preact = lax.psum_scatter(
        partial_value.astype(jnp.bfloat16), "chan", scatter_dimension=1, tiled=True
    ).astype(jnp.float32)
    output = jax.nn.silu(preact).astype(jnp.bfloat16)
    slopes_own = (cotangent.astype(jnp.float32) * silu_slope(preact)).astype(jnp.bfloat16)
    slopes_all = lax.all_gather(slopes_own, "chan", axis=1, tiled=True)
    grad_terms = lax.dot_general(
        joined, slopes_all, (((0,), (0,)), ((), ())), preferred_element_type=jnp.float32
    )
    grad_sums = lax.psum(grad_terms, "dom") * (1.0 / math.sqrt(float(node_rows * domains)))
    grad_self = grad_sums[:channels]
    grad_neigh = grad_sums[channels:]
    backward = lax.dot_general(
        slopes_all, weights, (((1,), (1,)), ((), ())), preferred_element_type=jnp.float32
    )
    back_self = backward[:, :channels]
    back_rows = (backward[:, channels:] / divisor).astype(jnp.bfloat16)
    back_blocks = back_rows.reshape(block_count, TILE, channels)
    returning = jnp.take(back_blocks.reshape(block_count, TILE * channels), got_index, axis=0)
    returned = lax.all_to_all(
        returning.reshape(domains, CAP * TILE * channels),
        "dom",
        split_axis=0,
        concat_axis=0,
        tiled=True,
    )
    returned = returned.reshape(slot_count, TILE, channels)
    remote_rows = jnp.take(returned, slot_index, axis=0)
    remote_terms = jnp.einsum(
        "tij,tjc->tic", remote_tiles, remote_rows, preferred_element_type=jnp.float32
    )
    onehot_remote = (
        jnp.arange(block_count, dtype=jnp.int32)[:, None] == remote_src[None, :]
    ).astype(jnp.float32)
    remote_back = jnp.einsum(
        "bt,tk->bk",
        onehot_remote,
        remote_terms.reshape(remote_count, -1),
        precision=lax.Precision.HIGHEST,
    )
    local_rows = jnp.take(back_blocks, local_dst, axis=0)
    local_terms = jnp.einsum(
        "tij,tjc->tic", local_tiles, local_rows, preferred_element_type=jnp.float32
    )
    onehot_local = (jnp.arange(block_count, dtype=jnp.int32)[:, None] == local_src[None, :]).astype(
        jnp.float32
    )
    local_back = jnp.einsum(
        "bt,tk->bk",
        onehot_local,
        local_terms.reshape(local_terms.shape[0], -1),
        precision=lax.Precision.HIGHEST,
    )
    gathered = (remote_back + local_back).reshape(node_rows, channels)
    grad_features = (back_self + gathered).astype(jnp.bfloat16)
    return (output, grad_self, grad_neigh, grad_features)


def solution(mesh):
    in_specs = (
        P("dom", "chan"),
        P("chan", None),
        P("chan", None),
        P("dom"),
        P("dom"),
        P("dom"),
        P("dom", None, None),
        P("dom"),
        P("dom", None),
        P("dom"),
        P("dom", None, None),
        P("dom", "chan"),
    )
    out_specs = (P("dom", "chan"), P("chan", None), P("chan", None), P("dom", "chan"))
    return jax.shard_map(
        per_device, mesh=mesh, in_specs=in_specs, out_specs=out_specs, check_vma=False
    )
```

profile of v0, /device:TPU:0, one launch (start us, length us, event | category | flops | bytes accessed | tf_op | source)
XLA Modules:
  0.0 361.2 jit_solution(5732093317905515113)
XLA Ops:
  10.2 8.3 %all-to-all-start = ((s32[16,1,2]{2,1,0:T(1,128)}), s32[16,1,2]{2,1,0:T(1,128)S(1)}, u32[]{:S(2)}, u32[]{:S(2)}) async-start(s32[16,1,2]{2,1,0:T(1,128)} %bitcast.5), calls=%async_computation | async-start | bytes 16384 | tf_op jit(solution)/shard_map/all_to_all | solution.py:34
  19.9 5.9 %all-to-all-done = s32[16,1,2]{2,1,0:T(1,128)S(1)} async-done(((s32[16,1,2]{2,1,0:T(1,128)}), s32[16,1,2]{2,1,0:T(1,128)S(1)}, u32[]{:S(2)}, u32[]{:S(2)}) %all-to-all-start) | async-done | bytes 160 | tf_op jit(solution)/shard_map/all_to_all | solution.py:34
  29.8 3.4 scatter_custom_fusion.1
  33.2 4.4 %all_to_all.21 = bf16[16,1,65536]{2,1,0:T(2,128)(2,1)} reshape(bf16[32,32768]{1,0:T(8,128)(2,1)S(1)} %scatter_custom_fusion.1) | data formatting | bytes 4194304 | tf_op jit(solution)/shard_map/all_to_all | solution.py:33
  38.0 12.9 %reduce.8 = bf16[16,65536]{1,0:T(8,128)(2,1)S(1)} reduce(bf16[16,1,65536]{2,1,0:T(2,128)(2,1)} %all_to_all.21, bf16[]{:T(256)} %broadcast.165), dimensions={1}, to_apply=%all_to_all.21.reduce_sub_computation | reduce | bytes 4194306 | tf_op jit(solution)/shard_map/all_to_all | solution.py:33
  51.0 2.8 reshape.226
  53.8 3.8 %all-to-all-start.1 = ((bf16[16,2,32768]{2,1,0:T(2,128)(2,1)}), bf16[16,2,32768]{2,1,0:T(2,128)(2,1)S(1)}, u32[]{:S(2)}, u32[]{:S(2)}) async-start(bf16[16,2,32768]{2,1,0:T(2,128)(2,1)} %reshape.226), calls=%async_computation.1 | async-start | bytes 4194304 | tf_op jit(solution)/shard_map/all_to_all | solution.py:33
  70.5 29.3 %all-to-all-done.1 = bf16[16,2,32768]{2,1,0:T(2,128)(2,1)S(1)} async-done(((bf16[16,2,32768]{2,1,0:T(2,128)(2,1)}), bf16[16,2,32768]{2,1,0:T(2,128)(2,1)S(1)}, u32[]{:S(2)}, u32[]{:S(2)}) %all-to-all-start.1) | async-done | bytes 2097184 | tf_op jit(solution)/shard_map/all_to_all | solution.py:33
  99.9 6.7 %reshape.227 = bf16[16,1,65536]{2,1,0:T(2,128)(2,1)} reshape(bf16[16,2,32768]{2,1,0:T(2,128)(2,1)S(1)} %all-to-all-done.1) | data formatting | bytes 4194304
  106.6 12.4 %reduce.1 = bf16[16,65536]{1,0:T(8,128)(2,1)S(1)} reduce(bf16[16,1,65536]{2,1,0:T(2,128)(2,1)} %reshape.227, bf16[]{:T(256)} %constant.72), dimensions={1}, to_apply=%all_to_all.19.reduce_sub_computation | reduce | bytes 4194306 | tf_op jit(solution)/shard_map/all_to_all | solution.py:33
  124.3 2.8 convolution_convert_fusion
  127.3 12.4 %reduce-scatter.2.cloned.1.call-done = bf16[1024,256]{1,0:T(8,128)(2,1)} async-done(((bf16[1024,512]{1,0:T(8,128)(2,1)}), bf16[1024,256]{1,0:T(8,128)(2,1)}) %reduce-scatter.2.cloned.1.call-update) | async-done | bytes 524304 | tf_op jit(solution)/shard_map/reduce_scatter | solution.py:83
  143.6 3.9 %broadcast_in_dim.81 = pred[16,1,65536]{2,0,1:T(8,128)(4,1)} reshape(pred[16,2,32768]{2,1,0:T(4,128)(4,1)S(1)} %broadcast_in_dim.80) | data formatting | bytes 2097152 | tf_op jit(solution)/shard_map/jit(_take)/broadcast_in_dim | solution.py:101
  147.5 4.8 %all-gather.2.cloned.1.call-done = bf16[1024,512]{1,0:T(8,128)(2,1)} async-done(((bf16[1024,256]{1,0:T(8,128)(2,1)}), bf16[1024,512]{1,0:T(8,128)(2,1)}) %all-gather.2.cloned.1.call-update) | async-done | bytes 1048592 | tf_op jit(solution)/shard_map/all_gather | solution.py:88
  162.8 2.8 reduce.9
  165.6 4.0 %reshape.228 = bf16[16,2,32768]{2,1,0:T(2,128)(2,1)} reshape(bf16[16,65536]{1,0:T(8,128)(2,1)} %reduce.9) | data formatting | bytes 4194304
  169.6 7.0 %all-to-all-start.2 = ((bf16[16,2,32768]{2,1,0:T(2,128)(2,1)}), bf16[16,2,32768]{2,1,0:T(2,128)(2,1)S(1)}, u32[]{:S(2)}, u32[]{:S(2)}) async-start(bf16[16,2,32768]{2,1,0:T(2,128)(2,1)} %reshape.228), calls=%async_computation.3 | async-start | bytes 4194304 | tf_op jit(solution)/shard_map/all_to_all | solution.py:102
  176.9 3.1 fusion.17
  183.1 2.6 copy.65
  185.7 2.8 copy.73
  188.5 127.0 %all-reduce.2.cloned.1.call-done = f32[512,512]{1,0:T(8,128)} async-done(((f32[512,512]{1,0:T(8,128)}), f32[512,512]{1,0:T(8,128)}) %all-reduce.2.cloned.1.call-update) | async-done | bytes 1048592 | tf_op jit(solution)/shard_map/psum | solution.py:92
  317.9 6.7 %reshape.229 = bf16[16,1,65536]{2,1,0:T(2,128)(2,1)} reshape(bf16[16,2,32768]{2,1,0:T(2,128)(2,1)S(1)} %all-to-all-done.2) | data formatting | bytes 4194304
  324.6 12.4 %reduce.3 = bf16[16,65536]{1,0:T(8,128)(2,1)S(1)} reduce(bf16[16,1,65536]{2,1,0:T(2,128)(2,1)} %reshape.229, bf16[]{:T(256)} %constant.72), dimensions={1}, to_apply=%all_to_all.20.reduce_sub_computation | reduce | bytes 4194306 | tf_op jit(solution)/shard_map/all_to_all | solution.py:102
  339.0 3.2 gather_fusion.2
  (95 shorter events, 61.6 us)
Async XLA Ops:
  7.2 20.4 %copy-start = (bf16[16,128,128]{2,1,0:T(8,128)(2,1)S(1)}, bf16[16,128,128]{2,1,0:T(8,128)(2,1)}, u32[]{:S(2)}) copy-start(bf16[16,128,128]{2,1,0:T(8,128)(2,1)} %param.24) | copy-start | bytes 1572868
  10.2 15.6 %all-to-all-start = ((s32[16,1,2]{2,1,0:T(1,128)}), s32[16,1,2]{2,1,0:T(1,128)S(1)}, u32[]{:S(2)}, u32[]{:S(2)}) async-start(s32[16,1,2]{2,1,0:T(1,128)} %bitcast.5), calls=%async_computation | async-start | bytes 16384 | tf_op jit(solution)/shard_map/all_to_all | solution.py:34
  53.8 4.1 %copy-start.15 = (s32[8]{0:T(128)S(1)}, s32[8]{0:T(128)}, u32[]{:S(2)}) copy-start(s32[8]{0:T(128)} %param.18) | copy-start | bytes 100
  53.8 4.1 %copy-start.3 = (bf16[1024,256]{1,0:T(8,128)(2,1)S(1)}, bf16[1024,256]{1,0:T(8,128)(2,1)}, u32[]{:S(2)}) copy-start(bf16[1024,256]{1,0:T(8,128)(2,1)} %param.14) | copy-start | bytes 1572868
  53.8 5.5 %copy-start.7 = (bf16[8,128,128]{2,1,0:T(8,128)(2,1)S(1)}, bf16[8,128,128]{2,1,0:T(8,128)(2,1)}, u32[]{:S(2)}) copy-start(bf16[8,128,128]{2,1,0:T(8,128)(2,1)} %param.20) | copy-start | bytes 786436
  53.8 46.1 %all-to-all-start.1 = ((bf16[16,2,32768]{2,1,0:T(2,128)(2,1)}), bf16[16,2,32768]{2,1,0:T(2,128)(2,1)S(1)}, u32[]{:S(2)}, u32[]{:S(2)}) async-start(bf16[16,2,32768]{2,1,0:T(2,128)(2,1)} %reshape.226), calls=%async_computation.1 | async-start | bytes 4194304 | tf_op jit(solution)/shard_map/all_to_all | solution.py:33
  57.6 82.1 %reduce-scatter.2.cloned.1.call-start = ((), (), s32[]{:S(2)}) async-start(), calls=%async_computation.4 | async-start | bytes 1572864 | tf_op jit(solution)/shard_map/reduce_scatter | solution.py:83
  61.8 4.5 %copy-start.12 = (s32[1024]{0:T(1024)S(1)}, s32[1024]{0:T(1024)}, u32[]{:S(2)}) copy-start(s32[1024]{0:T(1024)} %param.17) | copy-start | bytes 12292
  64.3 1.9 copy-start.10
  64.3 2.7 copy-start.11
  64.3 3.4 copy-start.13
  123.5 0.8 copy-start.8
  124.3 15.5 %copy-start.9 = (bf16[1024,256]{1,0:T(8,128)(2,1)S(1)}, bf16[1024,256]{1,0:T(8,128)(2,1)}, u32[]{:S(2)}) copy-start(bf16[1024,256]{1,0:T(8,128)(2,1)} %param.25) | copy-start | bytes 1572868
  127.1 25.3 %all-gather.2.cloned.1.call-start = ((), (), s32[]{:S(2)}) async-start(), calls=%async_computation.5 | async-start | bytes 1572864 | tf_op jit(solution)/shard_map/all_gather | solution.py:88
  154.5 1.3 copy-start.1
  156.0 0.8 copy-start.5
  169.6 7.3 %copy-start.4 = (bf16[1024,256]{1,0:T(8,128)(2,1)S(1)}, bf16[1024,256]{1,0:T(8,128)(2,1)}, u32[]{:S(2)}) copy-start(bf16[1024,256]{1,0:T(8,128)(2,1)} %param.14) | copy-start | bytes 1572868
  169.6 148.3 %all-to-all-start.2 = ((bf16[16,2,32768]{2,1,0:T(2,128)(2,1)}), bf16[16,2,32768]{2,1,0:T(2,128)(2,1)S(1)}, u32[]{:S(2)}, u32[]{:S(2)}) async-start(bf16[16,2,32768]{2,1,0:T(2,128)(2,1)} %reshape.228), calls=%async_computation.3 | async-start | bytes 4194304 | tf_op jit(solution)/shard_map/all_to_all | solution.py:102
  176.6 139.0 %all-reduce.2.cloned.1.call-start = ((), (), s32[]{:S(2)}) async-start(), calls=%async_computation.6 | async-start | bytes 2097152 | tf_op jit(solution)/shard_map/psum | solution.py:92
  344.0 2.0 copy-start.14
  346.0 2.5 copy-start.6
  348.5 4.0 %copy-start.2 = (f32[1024,512]{1,0:T(8,128)S(1)}, f32[1024,512]{1,0:T(8,128)}, u32[]{:S(2)}) copy-start(f32[1024,512]{1,0:T(8,128)} %copy-done.1) | copy-start | bytes 6291460
Sparse Core Ops, SparseCore 0:
  127.2 12.4 reduce-scatter.1
  142.4 9.9 all-gather.1
  182.6 132.8 all-reduce.1
where the time goes:
time: 362 us; the launch traced here: 361 us
  waiting for transfers between devices  180 us (50%)
  local copies, waits for them, and re-layouts  72.9 us (20%)
  other arithmetic  52.6 us (15%)
  matrix products  22.1 us (6%)
  starting transfers between devices  19.9 us (5%)
  between operations  14.1 us (4%)
    psum x1, waiting for transfers between devices, per_device(): lax.psum(grad_terms, 'dom') * (1.0 / math.sqrt(float(node_rows * domains)))  127 us
    unnamed x41, local copies, waits for them, and re-layouts  32.2 us
    all_to_all x1, waiting for transfers between devices, push_partials(): lax.all_to_all(outgoing, 'dom', split_axis=0, concat_axis=0, tiled=True)  29.3 us
    all_to_all x2, other arithmetic, push_partials(): lax.all_to_all(outgoing, 'dom', split_axis=0, concat_axis=0, tiled=True)  25.3 us
    reduce_scatter x1, waiting for transfers between devices, per_device(): lax.psum_scatter(partial_value.astype(jnp.bfloat16), 'chan', scatter_dime...  12.4 us
    all_to_all x1, other arithmetic, per_device(): lax.all_to_all(returning.reshape(domains, CAP * TILE * channels), 'dom',...  12.4 us
    all_to_all x1, starting transfers between devices, push_partials(): lax.all_to_all(out_blocks, 'dom', split_axis=0, concat_axis=0, tiled=True)  8.34 us
  transfers between devices with their start and end apart: 6, of which 5 were waited for; matrix products, arithmetic and copies ran while one was open for 9% of the time, Pallas kernels for 0%

commit v1 on v0

v1 whole, which is shorter than its diff:
```python
import math

import jax
import jax.numpy as jnp
from jax import lax
from jax.experimental import pallas as pl
from jax.experimental.pallas import tpu as pltpu
from jax.sharding import PartitionSpec as P

TILE = 128
CAP = 2
TAG_ROWS = 8
TAG_BITS = 4
TAGS_PER_WORD = 3

F32 = jnp.float32
BF16 = jnp.bfloat16
VMEM = pl.BlockSpec(memory_space=pltpu.VMEM)
SMEM = pl.BlockSpec(memory_space=pltpu.SMEM)


def call(kernel, name, out_shape, in_specs, out_specs, scratch, flops, nbytes):
    return pl.pallas_call(
        kernel,
        out_shape=out_shape,
        in_specs=in_specs,
        out_specs=out_specs,
        scratch_shapes=scratch,
        name=name,
        compiler_params=pltpu.CompilerParams(vmem_limit_bytes=24 * 1024 * 1024),
        cost_estimate=pl.CostEstimate(flops=flops, bytes_accessed=nbytes, transcendentals=0),
    )


def dot_tn(a, b):
    return lax.dot_general(a, b, (((0,), (0,)), ((), ())), preferred_element_type=F32)


def dot_nn(a, b):
    return lax.dot_general(a, b, (((1,), (0,)), ((), ())), preferred_element_type=F32)


def dot_nt(a, b):
    return lax.dot_general(a, b, (((1,), (1,)), ((), ())), preferred_element_type=F32)


def clear_counts(count):
    for place in range(count.shape[0]):
        count[place] = 0


def next_slot(part, count, number):
    target = part[number]
    place = count[target]
    count[target] = place + 1
    return target, place


def push_kernel(src, part, dst, feat, tiles, out, count):
    clear_counts(count)
    rows = out.shape[1] - TAG_ROWS
    out[:, rows:, :] = jnp.zeros((out.shape[0], TAG_ROWS, out.shape[2]), BF16)
    row_at = lax.broadcasted_iota(jnp.int32, (TAG_ROWS, out.shape[2]), 0)
    for number in range(tiles.shape[0]):
        target, place = next_slot(part, count, number)
        product = dot_tn(tiles[number], feat[src[number]])
        start = pl.multiple_of(place * TILE, TILE)
        out[target, pl.ds(start, TILE), :] = product.astype(BF16)
        tag = (dst[number] + 1).astype(F32)
        old = out[target, rows:, :].astype(F32)
        out[target, rows:, :] = jnp.where(row_at == place, tag, old).astype(BF16)


def local_kernel(src, dst, feat, tiles, out):
    out[...] = jnp.zeros(out.shape, F32)
    for number in range(tiles.shape[0]):
        out[dst[number]] += dot_tn(tiles[number], feat[src[number]])


def read_tags(recv, got):
    domains = recv.shape[0]
    rows = recv.shape[1] - TAG_ROWS
    row_at = lax.broadcasted_iota(jnp.int32, (TAG_ROWS, recv.shape[2]), 0)
    unit = jnp.where(row_at == 0, 1.0, 0.0)
    for place in range(1, CAP):
        unit = jnp.where(row_at == place, float(1 << (TAG_BITS * place)), unit)
    width = TAG_BITS * CAP
    for first in range(0, domains, TAGS_PER_WORD):
        members = range(first, min(first + TAGS_PER_WORD, domains))
        word = jnp.zeros((TAG_ROWS, recv.shape[2]), F32)
        for member in members:
            scale = float(1 << (width * (member - first)))
            word = word + recv[member, rows:, :].astype(F32) * (unit * scale)
        packed = jnp.max(jnp.sum(word, axis=0, keepdims=True)).astype(jnp.int32)
        for member in members:
            for place in range(CAP):
                shift = width * (member - first) + TAG_BITS * place
                got[member * CAP + place] = ((packed >> shift) & (2**TAG_BITS - 1)) - 1


def mid_kernel(recv, local, feat, w_self, w_neigh, degrees, averaged, share, got, acc):
    read_tags(recv, got)
    acc[...] = local[...]
    for slot in range(recv.shape[0] * CAP):
        block = got[slot]

        @pl.when(block >= 0)
        def _():
            start = (slot % CAP) * TILE
            acc[block] += recv[slot // CAP, start : start + TILE, :].astype(F32)

    width = share.shape[2]
    for block in range(acc.shape[0]):
        at = slice(block * TILE, (block + 1) * TILE)
        mean = (acc[block] / degrees[at, :]).astype(BF16)
        averaged[at, :] = mean
        value = dot_nn(feat[block], w_self[...]) + dot_nn(mean, w_neigh[...])
        value = value.astype(BF16)
        for piece in range(share.shape[0]):
            share[piece, at, :] = value[:, piece * width : (piece + 1) * width]


def silu_kernel(*refs):
    shares, cotangent, output, slopes = refs[:-3], refs[-3], refs[-2], refs[-1]
    step = TILE
    for start in range(0, output.shape[0], step):
        at = slice(start, start + step)
        value = shares[0][at, :].astype(F32)
        for piece in shares[1:]:
            value = value + piece[at, :].astype(F32)
        gate = 1.0 / (1.0 + jnp.exp(-value))
        output[at, :] = (value * gate).astype(BF16)
        slope = gate * (1.0 + value * (1.0 - gate))
        slopes[at, :] = (cotangent[at, :].astype(F32) * slope).astype(BF16)


def back_kernel(*refs):
    got, w_neigh, degrees = refs[:3]
    slopes, back, returning = refs[3:-2], refs[-2], refs[-1]
    width = slopes[0].shape[1]
    for block in range(back.shape[0]):
        at = slice(block * TILE, (block + 1) * TILE)
        total = dot_nt(slopes[0][at, :], w_neigh[:, :width])
        for piece in range(1, len(slopes)):
            columns = slice(piece * width, (piece + 1) * width)
            total = total + dot_nt(slopes[piece][at, :], w_neigh[:, columns])
        back[block] = (total / degrees[at, :]).astype(BF16)
    for slot in range(returning.shape[0] * CAP):
        block = got[slot]

        @pl.when(block >= 0)
        def _():
            start = (slot % CAP) * TILE
            returning[slot // CAP, start : start + TILE, :] = back[block]


def grads_kernel(*refs):
    feat, averaged, slopes, out = refs[0], refs[1], refs[2:-1], refs[-1]
    channels = feat.shape[1]
    width = slopes[0].shape[1]
    for piece, slope in enumerate(slopes):
        columns = slice(piece * width, (piece + 1) * width)
        out[:channels, columns] = dot_tn(feat[...], slope[...])
        out[channels:, columns] = dot_tn(averaged[...], slope[...])


def local_back_kernel(*refs):
    src, dst, tiles, back, w_self = refs[:5]
    slopes, out = refs[5:-1], refs[-1]
    width = slopes[0].shape[1]
    for block in range(out.shape[0]):
        at = slice(block * TILE, (block + 1) * TILE)
        total = dot_nt(slopes[0][at, :], w_self[:, :width])
        for piece in range(1, len(slopes)):
            columns = slice(piece * width, (piece + 1) * width)
            total = total + dot_nt(slopes[piece][at, :], w_self[:, columns])
        out[block] = total
    for number in range(tiles.shape[0]):
        out[src[number]] += dot_nn(tiles[number], back[dst[number]])


def final_kernel(src, part, tiles, returned, partial, out, count, acc):
    clear_counts(count)
    acc[...] = partial[...]
    for number in range(tiles.shape[0]):
        target, place = next_slot(part, count, number)
        start = pl.multiple_of(place * TILE, TILE)
        acc[src[number]] += dot_nn(tiles[number], returned[target, pl.ds(start, TILE), :])
    for block in range(acc.shape[0]):
        out[block] = acc[block].astype(BF16)


def shift_pairs(count, shift):
    return [(at, (at + shift) % count) for at in range(count)]


def reduce_over(value, axis):
    count = lax.axis_size(axis)
    here = lax.axis_index(axis)
    bits = count.bit_length() - 1
    rows, columns = value.shape
    sizes = []
    for bit in range(bits):
        half = value.shape[0] // 2
        upper = (here >> bit) & 1
        low, high = value[:half], value[half:]
        keep = jnp.where(upper == 1, high, low)
        send = jnp.where(upper == 1, low, high).astype(BF16)
        pairs = [(at, at ^ (1 << bit)) for at in range(count)]
        arrived = lax.ppermute(send, axis, pairs)
        value = keep + arrived.astype(F32)
    value = value.astype(BF16)
    for bit in reversed(range(bits)):
        upper = (here >> bit) & 1
        pairs = [(at, at ^ (1 << bit)) for at in range(count)]
        arrived = lax.ppermute(value, axis, pairs)
        low = jnp.where(upper == 1, arrived, value)
        high = jnp.where(upper == 1, value, arrived)
        value = jnp.concatenate([low, high], axis=0)
    return value.astype(F32)


def rotate_columns(weights, pieces, me):
    rows, columns = weights.shape
    double = jnp.concatenate([weights, weights], axis=1)
    return lax.dynamic_slice(double, (0, me * (columns // pieces)), (rows, columns))


def per_device(
    features,
    w_self,
    w_neigh,
    degrees,
    local_src,
    local_dst,
    local_tiles,
    remote_src,
    remote_part,
    remote_dst,
    remote_tiles,
    cotangent,
):
    domains = lax.axis_size("dom")
    shards = lax.axis_size("chan")
    me = lax.axis_index("chan")
    node_rows, channels = features.shape
    out_width = w_self.shape[1]
    own_width = out_width // shards
    blocks = node_rows // TILE
    rows = CAP * TILE
    n_remote, n_local = remote_tiles.shape[0], local_tiles.shape[0]
    feat_blocks = features.reshape(blocks, TILE, channels)
    targets = remote_part[:, 0]
    shape = jax.ShapeDtypeStruct
    tile_flops = 2 * TILE * TILE * channels
    block_bytes = 2 * TILE * channels

    outgoing = call(
        push_kernel,
        "push",
        shape((domains, rows + TAG_ROWS, channels), BF16),
        [SMEM, SMEM, SMEM, VMEM, VMEM],
        VMEM,
        [pltpu.SMEM((domains,), jnp.int32)],
        n_remote * tile_flops,
        (blocks + domains * CAP) * block_bytes,
    )(remote_src, targets, remote_dst, feat_blocks, remote_tiles)
    received = lax.all_to_all(outgoing, "dom", split_axis=0, concat_axis=0, tiled=True)

    local = call(
        local_kernel,
        "local",
        shape((blocks, TILE, channels), F32),
        [SMEM, SMEM, VMEM, VMEM],
        VMEM,
        [],
        n_local * tile_flops,
        3 * blocks * block_bytes,
    )(local_src, local_dst, feat_blocks, local_tiles)
    divisor = degrees.astype(F32)[:, None]
    own_self = rotate_columns(w_self, shards, me)
    own_neigh = rotate_columns(w_neigh, shards, me)

    averaged, share, got = call(
        mid_kernel,
        "mid",
        (
            shape((node_rows, channels), BF16),
            shape((shards, node_rows, own_width), BF16),
            shape((domains * CAP,), jnp.int32),
        ),
        [VMEM] * 6,
        (VMEM, VMEM, SMEM),
        [pltpu.VMEM((blocks, TILE, channels), F32)],
        4 * node_rows * channels * out_width,
        (domains * CAP + 4 * blocks) * block_bytes,
    )(received, local, feat_blocks, own_self, own_neigh, divisor)

    pieces = [share[0]]
    for shift in range(1, shards):
        pieces.append(lax.ppermute(share[shift], "chan", shift_pairs(shards, shift)))
    output, slopes_own = call(
        silu_kernel,
        "silu",
        (shape((node_rows, own_width), BF16), shape((node_rows, own_width), BF16)),
        [VMEM] * (shards + 1),
        (VMEM, VMEM),
        [],
        20 * node_rows * own_width,
        10 * node_rows * own_width,
    )(*pieces, cotangent)
    slopes = [slopes_own]
    for block in range(1, shards):
        pairs = shift_pairs(shards, shards - block)
        slopes.append(lax.ppermute(slopes_own, "chan", pairs))

    back, returning = call(
        back_kernel,
        "back",
        (shape((blocks, TILE, channels), BF16), shape((domains, rows, channels), BF16)),
        [SMEM, VMEM, VMEM] + [VMEM] * shards,
        (VMEM, VMEM),
        [],
        2 * node_rows * channels * out_width,
        (domains * CAP + 4 * blocks) * block_bytes,
    )(got, own_neigh, divisor, *slopes)
    returned = lax.all_to_all(returning, "dom", split_axis=0, concat_axis=0, tiled=True)

    grad_terms = call(
        grads_kernel,
        "grads",
        shape((2 * channels, out_width), F32),
        [VMEM] * (2 + shards),
        VMEM,
        [],
        4 * node_rows * channels * out_width,
        8 * node_rows * channels,
    )(features, averaged, *slopes)
    scale = 1.0 / math.sqrt(float(node_rows * domains))
    grad_sums = reduce_over(grad_terms, "dom") * scale
    grad_sums = rotate_columns(grad_sums, shards, (shards - me) % shards)

    partial = call(
        local_back_kernel,
        "local_back",
        shape((blocks, TILE, channels), F32),
        [SMEM, SMEM, VMEM, VMEM, VMEM] + [VMEM] * shards,
        VMEM,
        [],
        2 * node_rows * channels * out_width + n_local * tile_flops,
        8 * blocks * block_bytes,
    )(local_src, local_dst, local_tiles, back, own_self, *slopes)
    grad_features = call(
        final_kernel,
        "final",
        shape((blocks, TILE, channels), BF16),
        [SMEM, SMEM, VMEM, VMEM, VMEM],
        VMEM,
        [pltpu.SMEM((domains,), jnp.int32), pltpu.VMEM((blocks, TILE, channels), F32)],
        n_remote * tile_flops,
        (domains * CAP + 4 * blocks) * block_bytes,
    )(remote_src, targets, remote_tiles, returned, partial)
    return (
        output,
        grad_sums[:channels],
        grad_sums[channels:],
        grad_features.reshape(node_rows, channels),
    )


def solution(mesh):
    in_specs = (
        P("dom", "chan"),
        P("chan", None),
        P("chan", None),
        P("dom"),
        P("dom"),
        P("dom"),
        P("dom", None, None),
        P("dom"),
        P("dom", None),
        P("dom"),
        P("dom", None, None),
        P("dom", "chan"),
    )
    out_specs = (P("dom", "chan"), P("chan", None), P("chan", None), P("dom", "chan"))
    return jax.shard_map(
        per_device, mesh=mesh, in_specs=in_specs, out_specs=out_specs, check_vma=False
    )
```

time: 362 us -> 167 us (0.46)
  waiting for transfers between devices: 180 us -> 93.5 us
  local copies, waits for them, and re-layouts: 72.9 us -> 18.1 us
  other arithmetic: 52.6 us -> 12.4 us
  matrix products: 22.1 us -> 0 us
  between operations: 14.1 us -> 1.07 us
  starting transfers between devices: 19.9 us -> 30.7 us
  Pallas kernels: 0 us -> 10.1 us
    psum x1 -> x0, waiting for transfers between devices: 127 us -> none  [per_device(): lax.psum(grad_terms, 'dom') * (1.0 / math.sqrt(float(node_rows * domains)))]
    ppermute x0 -> x10, waiting for transfers between devices: none -> 53.5 us  [the longest x4 35.6 us: reduce_over(): arrived = lax.ppermute(send, axis, pairs)]
    all_to_all x4 -> x0, other arithmetic: 38.3 us -> none  [the longest x2 25.3 us: push_partials(): lax.all_to_all(outgoing, 'dom', split_axis=0, concat_axis=0, tiled=True)]
    dot_general x11 -> x0, matrix products: 22.1 us -> none  [the longest x1 3.11 us: per_device(): lax.dot_general(joined, slopes_all, (((0,), (0,)), ((), ())), preferred_e...]
    unnamed x41 -> x74, local copies, waits for them, and re-layouts: 32.2 us -> 16.8 us
    reduce_scatter x1 -> x0, waiting for transfers between devices: 12.4 us -> none  [per_device(): lax.psum_scatter(partial_value.astype(jnp.bfloat16), 'chan', scatter_dime...]
    gather x6 -> x0, local copies, waits for them, and re-layouts: 11.6 us -> none  [the longest x2 3.79 us: per_device(): jnp.take(back_blocks.reshape(block_count, TILE * channels), got_index, ax...]
    ppermute x0 -> x10, starting transfers between devices: none -> 11.6 us  [the longest x4 7.65 us: reduce_over(): arrived = lax.ppermute(send, axis, pairs)]
  transfers between devices with their start and end apart: 6 -> 12, of which waited for: 5 -> 10; matrix products, arithmetic and copies ran while one was open for 9% -> 8% of each run, Pallas kernels for 0% -> 2%
where the time goes in v1:
time: 167 us; the launch traced here: 166 us
  waiting for transfers between devices  93.5 us (56%)
  starting transfers between devices  30.7 us (18%)
  local copies, waits for them, and re-layouts  18.1 us (11%)
  other arithmetic  12.4 us (7%)
  Pallas kernels  10.1 us (6%)
    all_to_all x1, waiting for transfers between devices, per_device(): lax.all_to_all(outgoing, 'dom', split_axis=0, concat_axis=0, tiled=True)  40.1 us
    ppermute x4, waiting for transfers between devices, reduce_over(): arrived = lax.ppermute(send, axis, pairs)  35.6 us
    unnamed x74, local copies, waits for them, and re-layouts  16.8 us
    ppermute x4, waiting for transfers between devices, reduce_over(): arrived = lax.ppermute(value, axis, pairs)  14.2 us
    all_to_all x1, starting transfers between devices, per_device(): lax.all_to_all(returning, 'dom', split_axis=0, concat_axis=0, tiled=True)  10.6 us
    all_to_all x1, starting transfers between devices, per_device(): lax.all_to_all(outgoing, 'dom', split_axis=0, concat_axis=0, tiled=True)  8.48 us
    ppermute x4, starting transfers between devices, reduce_over(): arrived = lax.ppermute(send, axis, pairs)  7.65 us
    add x3, other arithmetic, reduce_over(): value = keep + arrived.astype(F32)  4.7 us
  transfers between devices with their start and end apart: 12, of which 10 were waited for; matrix products, arithmetic and copies ran while one was open for 8% of the time, Pallas kernels for 2%

profile of v1, /device:TPU:0, one launch (start us, length us, event | category | flops | bytes accessed | tf_op | source)
XLA Modules:
  0.0 165.9 jit_solution(5245993034057852523)
XLA Ops:
  5.7 1.4 copy-done
  7.1 8.5 %all-to-all-start = ((bf16[16,264,256]{2,1,0:T(8,128)(2,1)}), bf16[16,264,256]{2,1,0:T(8,128)(2,1)S(1)}, u32[]{:S(2)}, u32[]{:S(2)}) async-start(bf16[16,264,256]{2,1,0:T(8,128)(2,1)} %copy-done), calls=%async_computation | async-start | bytes 4325376 | tf_op jit(solution)/shard_map/all_to_all | solution.py:268
  17.8 1.9 %fusion.1 = (bf16[256,512]{1,0:T(8,128)(2,1)}, bf16[256,512]{1,0:T(8,128)(2,1)S(1)}) fusion(s32[]{:T(128)S(6)} %select_n.102, bf16[256,512]{1,0:T(8,128)(2,1)} %param.14, bf16[256,512]{1,0:T(8,128)(2,1)} %param.13), kind=kLoop, calls=%fused_computation.12 | loop fusion | flops 1048576 | bytes 1048580 | tf_op jit(solution)/shard_map/concatenate | solution.py:225
  19.7 40.1 %all-to-all-done.recv = bf16[16,264,256]{2,1,0:T(8,128)(2,1)S(1)} async-done(((bf16[16,264,256]{2,1,0:T(8,128)(2,1)}), bf16[16,264,256]{2,1,0:T(8,128)(2,1)S(1)}, u32[]{:S(2)}, u32[]{:S(2)}) %all-to-all-start) | async-done | bytes 2162720 | tf_op jit(solution)/shard_map/all_to_all | solution.py:268
  63.5 1.9 %collective-permute-done.refs_1_ = bf16[1024,256]{1,0:T(8,128)(2,1)S(1)} collective-permute-done((bf16[1024,256]{1,0:T(8,128)(2,1)S(1)}, bf16[1024,256]{1,0:T(8,128)(2,1)S(1)}, u32[]{:S(2)}, u32[]{:S(2)}) %collective-permute-start) | collective-permute-done | bytes 524320 | tf_op jit(solution)/shard_map/ppermute | solution.py:301
  66.6 1.8 %collective-permute-done.1.refs_3_.refs_4_.refs_6_ = bf16[1024,256]{1,0:T(8,128)(2,1)S(1)} collective-permute-done((bf16[1024,256]{1,0:T(8,128)(2,1)S(1)}, bf16[1024,256]{1,0:T(8,128)(2,1)S(1)}, u32[]{:S(2)}, u32[]{:S(2)}) %collective-permute-start.1) | collective-permute-done | bytes 524320 | tf_op jit(solution)/shard_map/ppermute | solution.py:315
  73.3 1.6 back.1
  75.0 1.3 copy-done.17
  77.1 10.6 %all-to-all-start.1 = ((bf16[16,256,256]{2,1,0:T(8,128)(2,1)}), bf16[16,256,256]{2,1,0:T(8,128)(2,1)S(1)}, u32[]{:S(2)}, u32[]{:S(2)}) async-start(bf16[16,256,256]{2,1,0:T(8,128)(2,1)} %copy-done.17), calls=%async_computation.1 | async-start | bytes 4194304 | tf_op jit(solution)/shard_map/all_to_all | solution.py:327
  87.8 1.9 %convert_add_fusion = f32[256,512]{1,0:T(8,128)} fusion(bf16[256,512]{1,0:T(8,128)(2,1)} %collective-permute-done.2, f32[512,512]{1,0:T(8,128)S(1)} %copy-done.4, pred[]{:T(512)S(6)} %eq.9), kind=kLoop, calls=%fused_computation.8 | loop fusion | flops 393216 | bytes 1835009 | tf_op jit(solution)/shard_map/add | solution.py:211
  89.6 1.8 %select_convert_fusion.1 = bf16[128,512]{1,0:T(8,128)(2,1)} fusion(f32[256,512]{1,0:T(8,128)} %convert_add_fusion, pred[]{:T(512)S(6)} %eq.10), kind=kLoop, calls=%fused_computation.16 | loop fusion | flops 65536 | bytes 393217 | tf_op jit(solution)/shard_map/convert_element_type | solution.py:208
  91.4 1.9 %collective-permute-start.3 = (bf16[128,512]{1,0:T(8,128)(2,1)}, bf16[128,512]{1,0:T(8,128)(2,1)}, u32[]{:S(2)}, u32[]{:S(2)}) collective-permute-start(bf16[128,512]{1,0:T(8,128)(2,1)} %select_convert_fusion.1), channel_id=1, source_target_pairs={{0,4},{2,6},{4,0},{6,2},{8,12},{10,14},{12,8},{14,10},{16,20},{18,... | collective-permute-start | bytes 393224 | tf_op jit(solution)/shard_map/ppermute | solution.py:210
  93.4 11.7 %collective-permute-done.3 = bf16[128,512]{1,0:T(8,128)(2,1)} collective-permute-done((bf16[128,512]{1,0:T(8,128)(2,1)}, bf16[128,512]{1,0:T(8,128)(2,1)}, u32[]{:S(2)}, u32[]{:S(2)}) %collective-permute-start.3) | collective-permute-done | bytes 131104 | tf_op jit(solution)/shard_map/ppermute | solution.py:210
  105.1 1.8 %convert_add_fusion.1 = f32[128,512]{1,0:T(8,128)} fusion(bf16[128,512]{1,0:T(8,128)(2,1)} %collective-permute-done.3, f32[256,512]{1,0:T(8,128)} %convert_add_fusion, pred[]{:T(512)S(6)} %eq.10), kind=kLoop, calls=%fused_computation.15 | loop fusion | flops 196608 | bytes 917505 | tf_op jit(solution)/shard_map/add | solution.py:211
  108.0 15.2 %collective-permute-done.4 = bf16[64,512]{1,0:T(8,128)(2,1)S(1)} collective-permute-done((bf16[64,512]{1,0:T(8,128)(2,1)S(1)}, bf16[64,512]{1,0:T(8,128)(2,1)S(1)}, u32[]{:S(2)}, u32[]{:S(2)}) %collective-permute-start.4) | collective-permute-done | bytes 65568 | tf_op jit(solution)/shard_map/ppermute | solution.py:210
  124.2 4.5 %collective-permute-start.5 = (bf16[32,512]{1,0:T(8,128)(2,1)S(1)}, bf16[32,512]{1,0:T(8,128)(2,1)S(1)}, u32[]{:S(2)}, u32[]{:S(2)}) collective-permute-start(bf16[32,512]{1,0:T(8,128)(2,1)S(1)} %select_convert_fusion.3), channel_id=1, source_target_pairs={{0,16},{2,18},{4,20},{6,22},{8,24},{10,26},{12,28},{14,30},{16,0},... | collective-permute-start | bytes 98312 | tf_op jit(solution)/shard_map/ppermute | solution.py:210
  128.7 8.6 %collective-permute-done.5 = bf16[32,512]{1,0:T(8,128)(2,1)S(1)} collective-permute-done((bf16[32,512]{1,0:T(8,128)(2,1)S(1)}, bf16[32,512]{1,0:T(8,128)(2,1)S(1)}, u32[]{:S(2)}, u32[]{:S(2)}) %collective-permute-start.5) | collective-permute-done | bytes 32800 | tf_op jit(solution)/shard_map/ppermute | solution.py:210
  137.4 4.8 %collective-permute-done.6 = bf16[32,512]{1,0:T(8,128)(2,1)S(1)} collective-permute-done((bf16[32,512]{1,0:T(8,128)(2,1)S(1)}, bf16[32,512]{1,0:T(8,128)(2,1)S(1)}, u32[]{:S(2)}, u32[]{:S(2)}) %collective-permute-start.6) | collective-permute-done | bytes 32800 | tf_op jit(solution)/shard_map/ppermute | solution.py:216
  142.4 4.3 %collective-permute-done.7 = bf16[64,512]{1,0:T(8,128)(2,1)S(1)} collective-permute-done((bf16[64,512]{1,0:T(8,128)(2,1)S(1)}, bf16[64,512]{1,0:T(8,128)(2,1)S(1)}, u32[]{:S(2)}, u32[]{:S(2)}) %collective-permute-start.7) | collective-permute-done | bytes 65568 | tf_op jit(solution)/shard_map/ppermute | solution.py:216
  146.7 2.6 %collective-permute-start.8 = (bf16[128,512]{1,0:T(8,128)(2,1)S(1)}, bf16[128,512]{1,0:T(8,128)(2,1)S(1)}, u32[]{:S(2)}, u32[]{:S(2)}) collective-permute-start(bf16[128,512]{1,0:T(8,128)(2,1)S(1)} %pad_maximum_fusion.1), channel_id=1, source_target_pairs={{0,4},{2,6},{4,0},{6,2},{8,12},{10,14},{12,8},{14,10},{16,20},{18,... | collective-permute-start | bytes 393224 | tf_op jit(solution)/shard_map/ppermute | solution.py:216
  149.2 2.9 %collective-permute-done.8 = bf16[128,512]{1,0:T(8,128)(2,1)S(1)} collective-permute-done((bf16[128,512]{1,0:T(8,128)(2,1)S(1)}, bf16[128,512]{1,0:T(8,128)(2,1)S(1)}, u32[]{:S(2)}, u32[]{:S(2)}) %collective-permute-start.8) | collective-permute-done | bytes 131104 | tf_op jit(solution)/shard_map/ppermute | solution.py:216
  156.6 1.5 local_back.1.partial
  158.1 2.2 %collective-permute-done.9 = bf16[256,512]{1,0:T(8,128)(2,1)} collective-permute-done((bf16[256,512]{1,0:T(8,128)(2,1)}, bf16[256,512]{1,0:T(8,128)(2,1)}, u32[]{:S(2)}, u32[]{:S(2)}) %collective-permute-start.9) | collective-permute-done | bytes 262176 | tf_op jit(solution)/shard_map/ppermute | solution.py:216
  164.1 1.8 %final.1 = bf16[8,128,256]{2,1,0:T(8,128)(2,1)} custom-call(s32[16]{0:T(128)S(1)} %copy-done.28, s32[16]{0:T(128)S(1)} %bitcast.12, bf16[16,128,128]{2,1,0:T(8,128)(2,1)S(1)} %copy-done.16, bf16[16,256,256]{2,1,0:T(8,128)(2,1)S(1)} %all-to-all-done.1.returned, f32[8,128,256]{2,1,0:T(8,128)S(1)} %copy-done.10), custom_call_target="tpu_custom_call" | custom-call | flops 134217728 | bytes 4194304 | tf_op jit(solution)/shard_map/final/pallas_call | solution.py:353
  (104 shorter events, 28.1 us)
Async XLA Ops:
  7.1 8.5 %copy-start.36 = (s32[1024]{0:T(1024)S(1)}, s32[1024]{0:T(1024)}, u32[]{:S(2)}) copy-start(s32[1024]{0:T(1024)} %param.15) | copy-start | bytes 12292
  7.1 8.8 %copy-start.2 = (bf16[1024,256]{1,0:T(8,128)(2,1)S(1)}, bf16[1024,256]{1,0:T(8,128)(2,1)}, u32[]{:S(2)}) copy-start(bf16[1024,256]{1,0:T(8,128)(2,1)} %refs_0_.2) | copy-start | bytes 1572868
  7.1 8.8 %copy-start.18 = (bf16[8,128,128]{2,1,0:T(8,128)(2,1)S(1)}, bf16[8,128,128]{2,1,0:T(8,128)(2,1)}, u32[]{:S(2)}) copy-start(bf16[8,128,128]{2,1,0:T(8,128)(2,1)} %refs_2_.3) | copy-start | bytes 786436
  7.1 8.8 %copy-start.25 = (s32[8]{0:T(128)S(1)}, s32[8]{0:T(128)}, u32[]{:S(2)}) copy-start(s32[8]{0:T(128)} %refs_0_.3) | copy-start | bytes 100
  7.1 8.8 %copy-start.26 = (s32[8]{0:T(128)S(1)}, s32[8]{0:T(128)}, u32[]{:S(2)}) copy-start(s32[8]{0:T(128)} %refs_1_.1) | copy-start | bytes 100
  7.1 52.6 %all-to-all-start = ((bf16[16,264,256]{2,1,0:T(8,128)(2,1)}), bf16[16,264,256]{2,1,0:T(8,128)(2,1)S(1)}, u32[]{:S(2)}, u32[]{:S(2)}) async-start(bf16[16,264,256]{2,1,0:T(8,128)(2,1)} %copy-done), calls=%async_computation | async-start | bytes 4325376 | tf_op jit(solution)/shard_map/all_to_all | solution.py:268
  63.4 2.0 %collective-permute-start = (bf16[1024,256]{1,0:T(8,128)(2,1)S(1)}, bf16[1024,256]{1,0:T(8,128)(2,1)S(1)}, u32[]{:S(2)}, u32[]{:S(2)}) collective-permute-start(bf16[1024,256]{1,0:T(8,128)(2,1)S(1)} %get-tuple-element.20), channel_id=1, source_target_pairs={{0,1},{1,0},{2,3},{3,2},{4,5},{5,4},{6,7},{7,6},{8,9},{9,8},{10,11... | collective-permute-start | bytes 1572872 | tf_op jit(solution)/shard_map/ppermute | solution.py:301
  66.5 8.4 %copy-start.5 = (bf16[1024,256]{1,0:T(8,128)(2,1)}, bf16[1024,256]{1,0:T(8,128)(2,1)S(1)}, u32[]{:S(2)}) copy-start(bf16[1024,256]{1,0:T(8,128)(2,1)S(1)} %get-tuple-element.14.refs_2_.refs_3_.refs_5_) | copy-start | bytes 1572868
  66.5 6.8 %copy-start.14 = (bf16[256,512]{1,0:T(8,128)(2,1)S(1)}, bf16[256,512]{1,0:T(8,128)(2,1)}, u32[]{:S(2)}) copy-start(bf16[256,512]{1,0:T(8,128)(2,1)} %get-tuple-element.30.w_neigh.refs_1_) | copy-start | bytes 786436
  66.5 1.9 %collective-permute-start.1 = (bf16[1024,256]{1,0:T(8,128)(2,1)S(1)}, bf16[1024,256]{1,0:T(8,128)(2,1)S(1)}, u32[]{:S(2)}, u32[]{:S(2)}) collective-permute-start(bf16[1024,256]{1,0:T(8,128)(2,1)S(1)} %get-tuple-element.14.refs_2_.refs_3_.refs_5_), channel_id=1, source_target_pairs={{0,1},{1,0},{2,3},{3,2},{4,5},{5,4},{6,7},{7,6},{8,9},{9,8},{10,11... | collective-permute-start | bytes 1572872 | tf_op jit(solution)/shard_map/ppermute | solution.py:315
  68.4 6.5 %copy-start.7 = (bf16[1024,256]{1,0:T(8,128)(2,1)}, bf16[1024,256]{1,0:T(8,128)(2,1)S(1)}, u32[]{:S(2)}) copy-start(bf16[1024,256]{1,0:T(8,128)(2,1)S(1)} %collective-permute-done.1.refs_3_.refs_4_.refs_6_) | copy-start | bytes 1572868
  72.1 15.6 %collective-permute-start.2 = (bf16[256,512]{1,0:T(8,128)(2,1)}, bf16[256,512]{1,0:T(8,128)(2,1)}, u32[]{:S(2)}, u32[]{:S(2)}) collective-permute-start(bf16[256,512]{1,0:T(8,128)(2,1)} %select_convert_fusion), channel_id=1, source_target_pairs={{0,2},{2,0},{4,6},{6,4},{8,10},{10,8},{12,14},{14,12},{16,18},{18,... | collective-permute-start | bytes 786440 | tf_op jit(solution)/shard_map/ppermute | solution.py:210
  77.1 10.7 %copy-start.4 = (f32[512,512]{1,0:T(8,128)S(1)}, f32[512,512]{1,0:T(8,128)}, u32[]{:S(2)}) copy-start(f32[512,512]{1,0:T(8,128)} %copy-done.3) | copy-start | bytes 3145732
  77.1 85.8 %all-to-all-start.1 = ((bf16[16,256,256]{2,1,0:T(8,128)(2,1)}), bf16[16,256,256]{2,1,0:T(8,128)(2,1)S(1)}, u32[]{:S(2)}, u32[]{:S(2)}) async-start(bf16[16,256,256]{2,1,0:T(8,128)(2,1)} %copy-done.17), calls=%async_computation.1 | async-start | bytes 4194304 | tf_op jit(solution)/shard_map/all_to_all | solution.py:327
  89.6 65.0 %copy-start.6 = (bf16[1024,256]{1,0:T(8,128)(2,1)S(1)}, bf16[1024,256]{1,0:T(8,128)(2,1)}, u32[]{:S(2)}) copy-start(bf16[1024,256]{1,0:T(8,128)(2,1)} %copy-done.5) | copy-start | bytes 1572868
  89.6 65.0 %copy-start.8 = (bf16[1024,256]{1,0:T(8,128)(2,1)S(1)}, bf16[1024,256]{1,0:T(8,128)(2,1)}, u32[]{:S(2)}) copy-start(bf16[1024,256]{1,0:T(8,128)(2,1)} %copy-done.7) | copy-start | bytes 1572868
  91.4 13.6 %collective-permute-start.3 = (bf16[128,512]{1,0:T(8,128)(2,1)}, bf16[128,512]{1,0:T(8,128)(2,1)}, u32[]{:S(2)}, u32[]{:S(2)}) collective-permute-start(bf16[128,512]{1,0:T(8,128)(2,1)} %select_convert_fusion.1), channel_id=1, source_target_pairs={{0,4},{2,6},{4,0},{6,2},{8,12},{10,14},{12,8},{14,10},{16,20},{18,... | collective-permute-start | bytes 393224 | tf_op jit(solution)/shard_map/ppermute | solution.py:210
  107.9 15.3 %collective-permute-start.4 = (bf16[64,512]{1,0:T(8,128)(2,1)S(1)}, bf16[64,512]{1,0:T(8,128)(2,1)S(1)}, u32[]{:S(2)}, u32[]{:S(2)}) collective-permute-start(bf16[64,512]{1,0:T(8,128)(2,1)S(1)} %select_convert_fusion.2), channel_id=1, source_target_pairs={{0,8},{2,10},{4,12},{6,14},{8,0},{10,2},{12,4},{14,6},{16,24},{18,... | collective-permute-start | bytes 196616 | tf_op jit(solution)/shard_map/ppermute | solution.py:210
  124.2 13.1 %collective-permute-start.5 = (bf16[32,512]{1,0:T(8,128)(2,1)S(1)}, bf16[32,512]{1,0:T(8,128)(2,1)S(1)}, u32[]{:S(2)}, u32[]{:S(2)}) collective-permute-start(bf16[32,512]{1,0:T(8,128)(2,1)S(1)} %select_convert_fusion.3), channel_id=1, source_target_pairs={{0,16},{2,18},{4,20},{6,22},{8,24},{10,26},{12,28},{14,30},{16,0},... | collective-permute-start | bytes 98312 | tf_op jit(solution)/shard_map/ppermute | solution.py:210
  137.4 4.9 %collective-permute-start.6 = (bf16[32,512]{1,0:T(8,128)(2,1)S(1)}, bf16[32,512]{1,0:T(8,128)(2,1)S(1)}, u32[]{:S(2)}, u32[]{:S(2)}) collective-permute-start(bf16[32,512]{1,0:T(8,128)(2,1)S(1)} %add_convert_fusion), channel_id=1, source_target_pairs={{0,16},{2,18},{4,20},{6,22},{8,24},{10,26},{12,28},{14,30},{16,0},... | collective-permute-start | bytes 98312 | tf_op jit(solution)/shard_map/ppermute | solution.py:216
  142.3 4.3 %collective-permute-start.7 = (bf16[64,512]{1,0:T(8,128)(2,1)S(1)}, bf16[64,512]{1,0:T(8,128)(2,1)S(1)}, u32[]{:S(2)}, u32[]{:S(2)}) collective-permute-start(bf16[64,512]{1,0:T(8,128)(2,1)S(1)} %pad_maximum_fusion.2), channel_id=1, source_target_pairs={{0,8},{2,10},{4,12},{6,14},{8,0},{10,2},{12,4},{14,6},{16,24},{18,... | collective-permute-start | bytes 196616 | tf_op jit(solution)/shard_map/ppermute | solution.py:216
  146.7 5.5 %collective-permute-start.8 = (bf16[128,512]{1,0:T(8,128)(2,1)S(1)}, bf16[128,512]{1,0:T(8,128)(2,1)S(1)}, u32[]{:S(2)}, u32[]{:S(2)}) collective-permute-start(bf16[128,512]{1,0:T(8,128)(2,1)S(1)} %pad_maximum_fusion.1), channel_id=1, source_target_pairs={{0,4},{2,6},{4,0},{6,2},{8,12},{10,14},{12,8},{14,10},{16,20},{18,... | collective-permute-start | bytes 393224 | tf_op jit(solution)/shard_map/ppermute | solution.py:216
  153.6 6.7 %collective-permute-start.9 = (bf16[256,512]{1,0:T(8,128)(2,1)}, bf16[256,512]{1,0:T(8,128)(2,1)}, u32[]{:S(2)}, u32[]{:S(2)}) collective-permute-start(bf16[256,512]{1,0:T(8,128)(2,1)} %pad_maximum_fusion), channel_id=1, source_target_pairs={{0,2},{2,0},{4,6},{6,4},{8,10},{10,8},{12,14},{14,12},{16,18},{18,... | collective-permute-start | bytes 786440 | tf_op jit(solution)/shard_map/ppermute | solution.py:216
  156.6 3.7 %copy-start.35 = (bf16[128,512]{1,0:T(8,128)(2,1)S(1)}, bf16[128,512]{1,0:T(8,128)(2,1)}, u32[]{:S(2)}) copy-start(bf16[128,512]{1,0:T(8,128)(2,1)} %copy-done.34) | copy-start | bytes 393220
  (25 other events, 34.9 us)
